TPU v7x, 256 devices: a whole 4x4x8 slice. The times are simulated.
256 devices in a mesh: layer: 8 (over z_hi, y), row: 32 (over x, z_lo, core).
Axes of the slice: x: 4, y: 4, z: 8 (z_hi: 2, z_lo: 4; z = z_hi * 4 + z_lo), core: 2. Of those that a mesh axis runs over, the one named last changes fastest.
Arguments:
- query_grads: bfloat16 [16, 1024, 4096], P('layer', 'row'), may hold values from -6 to 6
- train_grads: bfloat16 [16, 16384, 4096], P('layer', 'row'), may hold values from -0.023925781 to 0.023925781
- left_inverse: float32 [16, 64, 64], P('layer'), may hold values from -0.75 to 0.75
- right_inverse: float32 [16, 64, 64], P('layer'), may hold values from -0.75 to 0.75
Outputs:
- scores: float32 [1024, 16384], P('layer', 'row')
All inputs are finite; a program needn't handle non-finite values.
Results may differ from a plain program's by a relative error of at most 0.0029.
Values may be sent and summed in bfloat16 or wider, within the bound.
A program may use at most 128 MiB of HBM per device.

v0:
```python
import jax
import jax.numpy as jnp
from jax import lax
from jax.sharding import PartitionSpec as P


def on_device(query_grads, train_grads, left_inverse, right_inverse):
    layers, rows, feat = query_grads.shape
    proj = left_inverse.shape[1]
    square = query_grads.astype(jnp.float32).reshape(layers, rows, proj, proj)
    rotated = jnp.einsum(
        "lab,lqbc,lcd->lqad", left_inverse, square, right_inverse, precision=lax.Precision.HIGHEST
    )
    rotated = rotated.reshape(layers, rows, feat).astype(jnp.bfloat16)
    partial_value = jnp.einsum(
        "lqf,ltf->qt",
        lax.all_gather(rotated, "row", axis=1, tiled=True),
        train_grads,
        preferred_element_type=jnp.float32,
    )
    summed = lax.psum(partial_value, "layer")
    block = summed.shape[0] // lax.axis_size("layer")
    return lax.dynamic_slice_in_dim(summed, lax.axis_index("layer") * block, block, 0)


def solution(mesh):
    placed = (
        P("layer", "row", None),
        P("layer", "row", None),
        P("layer", None, None),
        P("layer", None, None),
    )
    return jax.shard_map(
        on_device, mesh=mesh, in_specs=placed, out_specs=P("layer", "row"), check_vma=False
    )
```

profile of v0, /device:TPU:24, one launch (start us, length us, event | category | flops | bytes accessed | tf_op | source)
XLA Modules:
  0.0 275.1 jit_solution(14499633773549307910)
XLA Ops:
  6.5 0.0 copy-start
  6.5 0.0 copy-start.1
  6.5 0.0 all-gather.2.cloned.1.call-start
  6.5 2.1 reshape.5
  8.6 0.0 copy-done
  8.6 1.0 fusion.1
  9.6 0.0 copy-done.1
  9.6 1.9 convolution_convert_fusion
  11.5 1.6 convert_element_type.8
  13.2 0.0 all-gather.2.cloned.1.call-update
  13.2 0.0 all-reduce.2.cloned.1.call-start
  13.2 102.5 %all-gather.2.cloned.1.call-done = bf16[2,1024,4096]{2,1,0:T(8,128)(2,1)} async-done(((bf16[2,32,4096]{2,1,0:T(8,128)(2,1)}), bf16[2,1024,4096]{2,1,0:T(8,128)(2,1)}) %all-gather.2.cloned.1.call-update) | async-done | bytes 16777232 | tf_op jit(solution)/shard_map/all_gather | solution.py:17
  115.7 15.8 %convolution_bitcast_fusion = f32[1024,512]{1,0:T(8,128)} fusion(bf16[2,1024,4096]{2,1,0:T(8,128)(2,1)} %all-gather.2.cloned.1.call-done, bf16[2,512,4096]{2,1,0:T(8,128)(2,1)} %param.5), kind=kOutput, calls=%fused_computation | convolution fusion | flops 8589934592 | bytes 27262976 | tf_op jit(solution)/shard_map/lqf,ltf->qt/dot_general | solution.py:15
  131.6 0.0 all-reduce.2.cloned.1.call-update
  131.6 135.0 %all-reduce.2.cloned.1.call-done = f32[1024,512]{1,0:T(8,128)} async-done(((f32[1024,512]{1,0:T(8,128)}), f32[1024,512]{1,0:T(8,128)}) %all-reduce.2.cloned.1.call-update) | async-done | bytes 2097168 | tf_op jit(solution)/shard_map/psum | solution.py:21
  266.6 1.7 constant_dynamic-slice_fusion
Async XLA Ops:
  6.5 2.1 copy-start
  6.5 3.1 %copy-start.1 = (f32[2,64,64]{2,1,0:T(8,128)S(1)}, f32[2,64,64]{2,1,0:T(8,128)}, u32[]{:S(2)}) copy-start(f32[2,64,64]{2,1,0:T(8,128)} %param.7) | copy-start | bytes 98308
  6.5 109.2 %all-gather.2.cloned.1.call-start = ((), (), s32[]{:S(2)}) async-start(), calls=%async_computation | async-start | bytes 17301504 | tf_op jit(solution)/shard_map/all_gather | solution.py:17
  13.2 253.4 %all-reduce.2.cloned.1.call-start = ((), (), s32[]{:S(2)}) async-start(), calls=%async_computation.1 | async-start | bytes 4194304 | tf_op jit(solution)/shard_map/psum | solution.py:21
Sparse Core Ops, SparseCore 0:
  13.3 102.3 all-gather.1
  131.7 134.8 all-reduce.1
where the time goes:
time: 275 us
  waiting for transfers between devices  238 us (87%)
  matrix products  18.7 us (7%)
  between operations  13.4 us (5%)
  local copies, waits for them, and re-layouts  5.38 us (2%)
    psum x1, waiting for transfers between devices, on_device(): summed = lax.psum(partial_value, 'layer')  135 us
    all_gather x1, waiting for transfers between devices, on_device(): lax.all_gather(rotated, 'row', axis=1, tiled=True)  102 us
    dot_general x1, matrix products, on_device(): jnp.einsum('lqf,ltf->qt', lax.all_gather(rotated, 'row', axis=1, tiled=Tr...  15.8 us
  transfers between devices with their start and end apart: 2, of which 2 were waited for; matrix products, arithmetic and copies ran while one was open for 0% of the time, Pallas kernels for 0%

commit v1 on v0

--- a/solution.py
+++ b/solution.py
@@ -2,6 +2,11 @@
 import jax.numpy as jnp
 from jax import lax
 from jax.sharding import PartitionSpec as P
+
+
+def exchange_gather(x, mesh_axis, dim):
+    sent = jnp.stack([x] * lax.axis_size(mesh_axis))
+    return jnp.concatenate(lax.all_to_all(sent, mesh_axis, 0, 0), axis=dim)
 
 
 def on_device(query_grads, train_grads, left_inverse, right_inverse):
@@ -14,7 +19,7 @@
     rotated = rotated.reshape(layers, rows, feat).astype(jnp.bfloat16)
     partial_value = jnp.einsum(
         "lqf,ltf->qt",
-        lax.all_gather(rotated, "row", axis=1, tiled=True),
+        exchange_gather(rotated, "row", 1),
         train_grads,
         preferred_element_type=jnp.float32,
     )

time: 275 us -> 552 us (2.01)
  blocking collectives: 0 us -> 374 us
  waiting for transfers between devices: 238 us -> 133 us
  local copies, waits for them, and re-layouts: 5.38 us -> 13.6 us
    all_to_all x0 -> x1, blocking collectives: none -> 374 us  [exchange_gather(): return jnp.concatenate(lax.all_to_all(sent, mesh_axis, 0, 0), axis=dim)]
    all_gather x1 -> x0, waiting for transfers between devices: 102 us -> none  [on_device(): lax.all_gather(rotated, 'row', axis=1, tiled=True)]
    reshape x0 -> x1, local copies, waits for them, and re-layouts: none -> 7.07 us  [exchange_gather(): return jnp.concatenate(lax.all_to_all(sent, mesh_axis, 0, 0), axis=dim)]
  transfers between devices with their start and end apart: 2 -> 1, of which waited for: 2 -> 1; matrix products, arithmetic and copies ran while one was open for 0% -> 0% of each run, Pallas kernels for 0% -> 0%
where the time goes in v1:
time: 552 us
  blocking collectives  374 us (68%)
  waiting for transfers between devices  133 us (24%)
  matrix products  18 us (3%)
  local copies, waits for them, and re-layouts  13.6 us (2%)
  between operations  13.5 us (2%)
    all_to_all x1, blocking collectives, exchange_gather(): return jnp.concatenate(lax.all_to_all(sent, mesh_axis, 0, 0), axis=dim)  374 us
    psum x1, waiting for transfers between devices, on_device(): summed = lax.psum(partial_value, 'layer')  133 us
    dot_general x1, matrix products, on_device(): jnp.einsum('lqf,ltf->qt', exchange_gather(rotated, 'row', 1), train_grads...  14.3 us
  transfers between devices with their start and end apart: 1, of which 1 were waited for; matrix products, arithmetic and copies ran while one was open for 0% of the time, Pallas kernels for 0%

profile of v1, /device:TPU:24, one launch (start us, length us, event | category | flops | bytes accessed | tf_op | source)
XLA Modules:
  0.0 551.6 jit_solution(18000130470132529813)
XLA Ops:
  6.5 0.0 copy-start
  6.5 0.0 all-reduce.2.cloned.1.call-start
  6.5 2.1 reshape.14
  8.6 0.0 copy-done
  8.6 1.0 fusion.1
  9.6 2.7 convolution_convert_fusion
  12.4 0.8 convert_element_type.10
  13.2 2.0 stack.2
  15.2 0.0 slice-start
  15.2 373.7 %all_to_all.5 = bf16[32,2,32,4096]{3,2,1,0:T(8,128)(2,1)S(1)} all-to-all(bf16[32,2,32,4096]{3,2,1,0:T(8,128)(2,1)S(1)} %stack.2), channel_id=1, replica_groups=mesh['layer'=8,'row'=32] {'row'}, dimensions={0} | all-to-all | bytes 33554432 | tf_op jit(solution)/shard_map/all_to_all | solution.py:9
  388.9 0.0 slice-start.1
  388.9 7.1 %copy.5 = bf16[2,32,32,4096]{3,2,1,0:T(8,128)(2,1)} copy(bf16[2,32,32,4096]{3,2,0,1:T(8,128)(2,1)S(1)} %bitcast.20) | data formatting | bytes 33554432 | tf_op jit(solution)/shard_map/reshape | solution.py:9
  396.0 0.0 slice-done
  396.0 0.0 slice-done.1
  396.0 0.0 copy-start.1
  396.0 14.3 %convolution_bitcast_fusion = f32[1024,512]{1,0:T(8,128)} fusion(bf16[2,1024,4096]{2,1,0:T(8,128)(2,1)} %bitcast.21, bf16[2,512,4096]{2,1,0:T(8,128)(2,1)S(1)} %bitcast.23), kind=kOutput, calls=%fused_computation | convolution fusion | flops 8589934592 | bytes 27262976 | tf_op jit(solution)/shard_map/lqf,ltf->qt/dot_general | solution.py:20
  410.3 0.0 all-reduce.2.cloned.1.call-update
  410.4 132.7 %all-reduce.2.cloned.1.call-done = f32[1024,512]{1,0:T(8,128)} async-done(((f32[1024,512]{1,0:T(8,128)}), f32[1024,512]{1,0:T(8,128)}) %all-reduce.2.cloned.1.call-update) | async-done | bytes 2097168 | tf_op jit(solution)/shard_map/psum | solution.py:26
  543.1 1.7 constant_dynamic-slice_fusion
  544.7 0.0 copy-done.1
  (1 shorter events, 0.0 us)
Async XLA Ops:
  6.5 2.1 copy-start
  6.5 536.5 %all-reduce.2.cloned.1.call-start = ((), (), s32[]{:S(2)}) async-start(), calls=%async_computation.1 | async-start | bytes 4194304 | tf_op jit(solution)/shard_map/psum | solution.py:26
  15.2 380.8 %slice-start = ((s8[8388608]{0:T(1024)(128)(4,1)}), s8[4194304]{0:T(1024)(128)(4,1)S(1)}, s32[]{:S(2)}) async-start(s8[8388608]{0:T(1024)(128)(4,1)} %bitcast.22), calls=%async_computation.2 | async-start | bytes 8388608
  388.9 7.1 %slice-start.1 = ((s8[8388608]{0:T(1024)(128)(4,1)}), s8[4194304]{0:T(1024)(128)(4,1)S(1)}, s32[]{:S(2)}) async-start(s8[8388608]{0:T(1024)(128)(4,1)} %bitcast.22), calls=%async_computation.3 | async-start | bytes 8388608
  396.0 148.7 %copy-start.1 = (f32[2,64,64]{2,1,0:T(8,128)S(1)}, f32[2,64,64]{2,1,0:T(8,128)}, u32[]{:S(2)}) copy-start(f32[2,64,64]{2,1,0:T(8,128)} %param.6) | copy-start | bytes 98308
Sparse Core Ops, SparseCore 0:
  410.5 132.5 all-reduce.1

commit v2 on v0

--- a/solution.py
+++ b/solution.py
@@ -18,7 +18,8 @@
         train_grads,
         preferred_element_type=jnp.float32,
     )
-    summed = lax.psum(partial_value, "layer")
+    parts = lax.all_gather(partial_value, "layer", axis=0, tiled=False)
+    summed = parts.sum(axis=0)
     block = summed.shape[0] // lax.axis_size("layer")
     return lax.dynamic_slice_in_dim(summed, lax.axis_index("layer") * block, block, 0)
 

time: 275 us -> 456 us (1.66)
  waiting for transfers between devices: 238 us -> 408 us
  other arithmetic: 0 us -> 8.08 us
    all_gather x0 -> x1, waiting for transfers between devices: none -> 306 us  [on_device(): parts = lax.all_gather(partial_value, 'layer', axis=0, tiled=False)]
    psum x1 -> x0, waiting for transfers between devices: 135 us -> none  [on_device(): summed = lax.psum(partial_value, 'layer')]
    reduce_sum x0 -> x1, other arithmetic: none -> 8.08 us  [on_device(): summed = parts.sum(axis=0)]
where the time goes in v2:
time: 456 us; the launch traced here: 453 us
  waiting for transfers between devices  408 us (89%)
  matrix products  18.7 us (4%)
  between operations  13.4 us (3%)
  other arithmetic  8.08 us (2%)
    all_gather x1, waiting for transfers between devices, on_device(): parts = lax.all_gather(partial_value, 'layer', axis=0, tiled=False)  306 us
    all_gather x1, waiting for transfers between devices, on_device(): lax.all_gather(rotated, 'row', axis=1, tiled=True)  102 us
    dot_general x1, matrix products, on_device(): jnp.einsum('lqf,ltf->qt', lax.all_gather(rotated, 'row', axis=1, tiled=Tr...  15.8 us
  transfers between devices with their start and end apart: 2, of which 2 were waited for; matrix products, arithmetic and copies ran while one was open for 0% of the time, Pallas kernels for 0%

profile of v2, /device:TPU:24, one launch (start us, length us, event | category | flops | bytes accessed | tf_op | source)
XLA Modules:
  0.0 453.2 jit_solution(7298761061838377699)
XLA Ops:
  6.5 0.0 copy-start
  6.5 0.0 copy-start.1
  6.5 0.0 all-gather.4.cloned.1.call-start
  6.5 2.1 reshape.5
  8.6 0.0 copy-done
  8.6 1.0 fusion.1
  9.6 0.0 copy-done.1
  9.6 1.9 convolution_convert_fusion
  11.5 1.6 convert_element_type.8
  13.2 0.0 all-gather.4.cloned.1.call-update
  13.2 0.0 all-gather.6.cloned.1.call-start
  13.2 102.5 %all-gather.4.cloned.1.call-done = bf16[2,1024,4096]{2,1,0:T(8,128)(2,1)} async-done(((bf16[2,32,4096]{2,1,0:T(8,128)(2,1)}), bf16[2,1024,4096]{2,1,0:T(8,128)(2,1)}) %all-gather.4.cloned.1.call-update) | async-done | bytes 16777232 | tf_op jit(solution)/shard_map/all_gather | solution.py:17
  115.7 15.8 %convolution_bitcast_fusion = f32[1024,512]{1,0:T(8,128)} fusion(bf16[2,1024,4096]{2,1,0:T(8,128)(2,1)} %all-gather.4.cloned.1.call-done, bf16[2,512,4096]{2,1,0:T(8,128)(2,1)} %param.5), kind=kOutput, calls=%fused_computation | convolution fusion | flops 8589934592 | bytes 27262976 | tf_op jit(solution)/shard_map/lqf,ltf->qt/dot_general | solution.py:15
  131.6 0.0 all-gather.6.cloned.1.call-update
  131.6 305.9 %all-gather.6.cloned.1.call-done = f32[8192,512]{1,0:T(8,128)} async-done(((f32[1024,512]{1,0:T(8,128)}), f32[8192,512]{1,0:T(8,128)}) %all-gather.6.cloned.1.call-update) | async-done | bytes 16777232 | tf_op jit(solution)/shard_map/all_gather | solution.py:21
  437.5 8.1 %reduce_sum.9 = f32[1024,512]{1,0:T(8,128)S(1)} reduce(f32[8,1024,512]{2,1,0:T(8,128)} %bitcast.19, f32[]{:T(128)} %constant.2.clone.1), dimensions={0}, to_apply=%region_0.0 | reduce | flops 3670016 | bytes 18874372 | tf_op jit(solution)/shard_map/reduce_sum | solution.py:22
  445.6 0.7 constant_dynamic-slice_fusion
Async XLA Ops:
  6.5 2.1 copy-start
  6.5 3.1 copy-start.1
  6.5 109.2 %all-gather.4.cloned.1.call-start = ((), (), s32[]{:S(2)}) async-start(), calls=%async_computation | async-start | bytes 17301504 | tf_op jit(solution)/shard_map/all_gather | solution.py:17
  13.2 424.3 %all-gather.6.cloned.1.call-start = ((), (), s32[]{:S(2)}) async-start(), calls=%async_computation.1 | async-start | bytes 18874368 | tf_op jit(solution)/shard_map/all_gather | solution.py:21
Sparse Core Ops, SparseCore 0:
  13.3 102.3 all-gather.3
  131.7 305.7 all-gather.5
